TPU v7x, 512 devices: a whole 4x8x8 slice. The times are simulated.
512 devices in a mesh: samp: 8 (over z), pair: 16 (over y_lo, x), recv: 4 (over y_hi, core).
Axes of the slice: x: 4, y: 8 (y_hi: 2, y_lo: 4; y = y_hi * 4 + y_lo), z: 8, core: 2. Of those that a mesh axis runs over, the one named last changes fastest.
Arguments:
- cell_expression: bfloat16 [32, 16384, 2048], P('samp', 'recv', 'pair'), may hold values from 0 to 24
- cell_labels: int32 [32, 16384], P('samp', 'recv'), may hold values from 0 to 127, as said below
- ligand_gene: int32 [2048], P('pair'), may hold values from 0 to 2047
- receptor_gene: int32 [2048], P('pair'), may hold values from 0 to 2047
- pair_factor: bfloat16 [2048, 32], P('pair'), may hold values from -0.53033009 to 0.53033009
- sender_factor: bfloat16 [128, 32], replicated, may hold values from -0.5 to 0.5
- receiver_factor: bfloat16 [128, 32], P('recv'), may hold values from -2.5 to 2.5
Outputs:
- sample_factor: float32 [32, 32], P('samp')
Inputs may be any that keep to these rules, and one draw needn't show every extreme that they name: `cell_labels`: in every sample one cell type has no cell.
All inputs are finite; a program needn't handle non-finite values.
Results may differ from a plain program's by a relative error of at most 0.0051.
Values may be sent and summed in bfloat16 or wider, within the bound.
No kernel may reach another device: no remote copies, remote signals or barrier semaphores. Data moves between devices by JAX's collectives and lax.ppermute only.
A program may use at most 64 MiB of HBM per device.

v0:
```python
import jax
import jax.numpy as jnp
from jax import lax
from jax.sharding import PartitionSpec as P


def body(
    cell_expression,
    cell_labels,
    ligand_gene,
    receptor_gene,
    pair_factor,
    sender_factor,
    receiver_factor,
):
    clusters = sender_factor.shape[0]
    factor_rank = sender_factor.shape[1]
    block_width = receiver_factor.shape[0]
    member = (
        cell_labels[:, :, None] == jnp.arange(clusters, dtype=jnp.int32)[None, None, :]
    ).astype(jnp.bfloat16)
    part_sums = jnp.einsum(
        "scg,sck->sgk", cell_expression, member, preferred_element_type=jnp.float32
    )
    part_counts = jnp.sum(member, axis=1, dtype=jnp.float32)
    receiver_start = lax.axis_index("recv") * block_width
    cluster_total, cell_count = lax.psum((part_sums, part_counts), "recv")
    cluster_mean = (cluster_total / jnp.maximum(cell_count, 1.0)[:, None, :]).astype(jnp.bfloat16)
    segment = lax.all_gather(cluster_mean, "pair", axis=1, tiled=True)
    ligand_table = jnp.einsum(
        "sga,ar->srg", segment, sender_factor, preferred_element_type=jnp.float32
    ).astype(jnp.bfloat16)
    receiver_columns = lax.dynamic_slice_in_dim(segment, receiver_start, block_width, 2)
    receptor_table = jnp.einsum(
        "sgb,br->srg", receiver_columns, receiver_factor, preferred_element_type=jnp.float32
    ).astype(jnp.bfloat16)
    joined_tables = jnp.concatenate([ligand_table, receptor_table], axis=1)
    ligand_rows = jnp.take(joined_tables[:, :factor_rank, :], ligand_gene, axis=2).astype(
        jnp.float32
    )
    receptor_rows = jnp.take(joined_tables[:, factor_rank:, :], receptor_gene, axis=2).astype(
        jnp.float32
    )
    pair_weights = pair_factor.astype(jnp.float32).T
    partial_product = jnp.sum(ligand_rows * receptor_rows * pair_weights[None, :, :], axis=2)
    pair_gram = jnp.einsum(
        "pr,pq->rq", pair_factor, pair_factor, preferred_element_type=jnp.float32
    )
    sender_gram = jnp.einsum(
        "pr,pq->rq", sender_factor, sender_factor, preferred_element_type=jnp.float32
    )
    receiver_gram = jnp.einsum(
        "pr,pq->rq", receiver_factor, receiver_factor, preferred_element_type=jnp.float32
    )
    product_total = lax.psum(partial_product, ("pair", "recv"))
    pair_gram = lax.psum(pair_gram, "pair")
    receiver_gram = lax.psum(receiver_gram, "recv")
    hadamard = pair_gram * sender_gram * receiver_gram
    cholesky_factor = jnp.linalg.cholesky(hadamard)
    solution = jax.scipy.linalg.cho_solve((cholesky_factor, True), product_total.T)
    return solution.T


def solution(mesh):
    placed = (
        P("samp", "recv", "pair"),
        P("samp", "recv"),
        P("pair"),
        P("pair"),
        P("pair", None),
        P(),
        P("recv", None),
    )
    return jax.shard_map(
        body, mesh=mesh, in_specs=placed, out_specs=P("samp", None), check_vma=False
    )
```

profile of v0, /device:TPU:9, one launch (start us, length us, event | category | flops | bytes accessed | tf_op | source)
XLA Modules:
  0.0 325.3 jit_solution(4889094992332328623)
XLA Ops:
  6.5 0.0 copy-start
  6.5 0.0 copy-start.2
  6.5 0.0 copy-start.3
  6.5 0.0 copy-start.1
  6.5 0.0 copy-start.4
  6.5 0.0 copy-start.5
  6.6 0.0 all-reduce.3.cloned.1.call-start
  6.6 4.6 %fusion.3 = f32[4,128,128]{1,2,0:T(8,128)} fusion(bf16[4,4096,128]{2,1,0:T(8,128)(2,1)} %param.9, s32[4,4096]{1,0:T(4,128)} %param.10), kind=kOutput, calls=%fused_computation.9 | convolution fusion | flops 538968064 | bytes 4521984 | tf_op jit(solution)/shard_map/scg,sck->sgk/dot_general | solution.py:22
  11.2 0.0 all-reduce.3.cloned.1.call-update
  11.2 0.0 all-gather.2.cloned.1.call-start
  11.3 0.0 copy-done.3
  11.3 0.2 fusion.16
  11.5 0.0 copy-done.2
  11.5 1.3 convert_reduce_fusion
  12.8 18.3 %all-reduce = (f32[4,128]{1,0:T(4,128)S(1)}, f32[32,32]{0,1:T(8,128)S(1)}) all-reduce(f32[4,128]{1,0:T(4,128)S(1)} %convert_reduce_fusion, f32[32,32]{0,1:T(8,128)S(1)} %fusion.16), channel_id=1, replica_groups=mesh['samp'=8,'pair'=16,'recv'=4] {'recv'}, use_global_device_ids=true, to_apply=%region_6.7 | all-reduce | flops 1536 | bytes 12288 | tf_op jit(solution)/shard_map/psum | solution.py:27
  31.0 43.7 %all-reduce.3.cloned.1.call-done = f32[4,128,128]{1,2,0:T(8,128)} async-done(((f32[4,128,128]{1,2,0:T(8,128)}), f32[4,128,128]{1,2,0:T(8,128)}) %all-reduce.3.cloned.1.call-update) | async-done | bytes 262160 | tf_op jit(solution)/shard_map/psum | solution.py:27
  74.7 1.7 divide_convert_fusion
  76.4 0.0 all-gather.2.cloned.1.call-update
  76.5 0.0 copy-done.1
  76.5 0.1 fusion.15
  76.6 57.9 %psum.35 = f32[32,32]{0,1:T(8,128)S(1)} all-reduce(f32[32,32]{0,1:T(8,128)S(1)} %fusion.15), channel_id=1, replica_groups=mesh['samp'=8,'pair'=16,'recv'=4] {'pair'}, use_global_device_ids=true, to_apply=%region_0.0 | all-reduce | flops 1024 | bytes 8192 | tf_op jit(solution)/shard_map/psum | solution.py:56
  134.5 0.0 copy-done
  134.5 0.1 fusion.4
  134.6 0.1 copy.16
  134.7 2.9 cholesky.16
  137.6 0.6 compare_reduce_fusion
  138.3 0.7 fusion.6
  138.9 2.5 custom-call.10
  141.4 0.1 copy.17
  141.5 0.0 copy-done.4
  141.5 0.0 copy-done.5
  141.6 0.3 all-gather.2.cloned.1.call-done
  141.8 2.0 convolution_convert_fusion
  143.8 1.4 copy.23
  145.2 1.4 convolution_convert_fusion.1
  146.6 2.5 copy.24
  149.1 0.7 gather_fusion
  149.9 2.3 gather_fusion.1
  152.2 0.3 multiply_reduce_fusion
  152.6 164.9 %psum.39 = f32[4,32]{1,0:T(4,128)S(1)} all-reduce(f32[4,32]{1,0:T(4,128)S(1)} %multiply_reduce_fusion), channel_id=1, replica_groups=mesh['samp'=8,'pair'=16,'recv'=4] {'pair','recv'}, use_global_device_ids=true, to_apply=%region_8.10 | all-reduce | flops 128 | bytes 1024 | tf_op jit(solution)/shard_map/psum | solution.py:55
  317.5 0.2 fusion.9
  317.7 0.8 fusion.7
  (9 shorter events, 0.1 us)
Async XLA Ops:
  6.5 127.9 %copy-start = (bf16[128,32]{0,1:T(8,128)(2,1)S(1)}, bf16[128,32]{0,1:T(8,128)(2,1)}, u32[]{:S(2)}) copy-start(bf16[128,32]{0,1:T(8,128)(2,1)} %param.14) | copy-start | bytes 24580
  6.5 4.9 %copy-start.2 = (s32[4,4096]{1,0:T(4,128)S(1)}, s32[4,4096]{1,0:T(4,128)}, u32[]{:S(2)}) copy-start(s32[4,4096]{1,0:T(4,128)} %param.10) | copy-start | bytes 196612
  6.5 4.7 %copy-start.3 = (bf16[32,32]{1,0:T(8,128)(2,1)S(1)}, bf16[32,32]{1,0:T(8,128)(2,1)}, u32[]{:S(2)}) copy-start(bf16[32,32]{1,0:T(8,128)(2,1)} %param.15) | copy-start | bytes 6148
  6.5 69.9 %copy-start.1 = (bf16[128,32]{0,1:T(8,128)(2,1)S(1)}, bf16[128,32]{0,1:T(8,128)(2,1)}, u32[]{:S(2)}) copy-start(bf16[128,32]{0,1:T(8,128)(2,1)} %param.13) | copy-start | bytes 24580
  6.5 134.9 %copy-start.4 = (s32[128]{0:T(128)S(1)}, s32[128]{0:T(128)}, u32[]{:S(2)}) copy-start(s32[128]{0:T(128)} %param.12) | copy-start | bytes 1540
  6.5 135.0 %copy-start.5 = (s32[128]{0:T(128)S(1)}, s32[128]{0:T(128)}, u32[]{:S(2)}) copy-start(s32[128]{0:T(128)} %param.11) | copy-start | bytes 1540
  6.6 68.1 %all-reduce.3.cloned.1.call-start = ((), (), s32[]{:S(2)}) async-start(), calls=%async_computation | async-start | bytes 524288 | tf_op jit(solution)/shard_map/psum | solution.py:27
  11.2 130.6 %all-gather.2.cloned.1.call-start = ((), (), s32[]{:S(2)}) async-start(), calls=%async_computation.1 | async-start | bytes 2228224 | tf_op jit(solution)/shard_map/all_gather | solution.py:29
Sparse Core Ops, SparseCore 0:
  11.3 63.2 all-reduce.2
  76.9 64.9 all-gather.1
where the time goes:
time: 326 us; the launch traced here: 325 us
  blocking collectives  241 us (74%)
  waiting for transfers between devices  43.9 us (13%)
  between operations  13.6 us (4%)
  other arithmetic  10.1 us (3%)
  matrix products  9.4 us (3%)
  local copies, waits for them, and re-layouts  7.17 us (2%)
    psum x1, blocking collectives, body(): product_total = lax.psum(partial_product, ('pair', 'recv'))  165 us
    psum x1, blocking collectives, body(): pair_gram = lax.psum(pair_gram, 'pair')  57.9 us
    psum x1, waiting for transfers between devices, body(): cluster_total, cell_count = lax.psum((part_sums, part_counts), 'recv')  43.7 us
    psum x1, blocking collectives, body(): cluster_total, cell_count = lax.psum((part_sums, part_counts), 'recv')  18.3 us
  transfers between devices with their start and end apart: 2, of which 2 were waited for; matrix products, arithmetic and copies ran while one was open for 3% of the time, Pallas kernels for 0%

commit v1 on v0

--- a/solution.py
+++ b/solution.py
@@ -53,7 +53,8 @@
         "pr,pq->rq", receiver_factor, receiver_factor, preferred_element_type=jnp.float32
     )
     product_total = lax.psum(partial_product, ("pair", "recv"))
-    pair_gram = lax.psum(pair_gram, "pair")
+    parts = lax.all_gather(pair_gram, "pair", axis=0, tiled=False)
+    pair_gram = parts.sum(axis=0)
     receiver_gram = lax.psum(receiver_gram, "recv")
     hadamard = pair_gram * sender_gram * receiver_gram
     cholesky_factor = jnp.linalg.cholesky(hadamard)

time: 326 us -> 323 us (level)
  the two profiles are of different devices: /device:TPU:9 before, /device:TPU:24 now
where the time goes in v1:
time: 323 us
  blocking collectives  208 us (64%)
  waiting for transfers between devices  74.4 us (23%)
  between operations  13.6 us (4%)
  other arithmetic  10.2 us (3%)
  matrix products  9.26 us (3%)
  local copies, waits for them, and re-layouts  7.24 us (2%)
    psum x1, blocking collectives, body(): product_total = lax.psum(partial_product, ('pair', 'recv'))  153 us
    psum x1, waiting for transfers between devices, body(): cluster_total, cell_count = lax.psum((part_sums, part_counts), 'recv')  38.7 us
    all_gather x1, waiting for transfers between devices, body(): segment = lax.all_gather(cluster_mean, 'pair', axis=1, tiled=True)  35.7 us
    all_gather x1, blocking collectives, body(): parts = lax.all_gather(pair_gram, 'pair', axis=0, tiled=False)  34.7 us
    psum x1, blocking collectives, body(): cluster_total, cell_count = lax.psum((part_sums, part_counts), 'recv')  20.8 us
  transfers between devices with their start and end apart: 2, of which 2 were waited for; matrix products, arithmetic and copies ran while one was open for 3% of the time, Pallas kernels for 0%

profile of v1, /device:TPU:24, one launch (start us, length us, event | category | flops | bytes accessed | tf_op | source)
XLA Modules:
  0.0 323.1 jit_solution(1918330318000444838)
XLA Ops:
  6.5 0.0 copy-start
  6.5 0.0 copy-start.2
  6.5 0.0 copy-start.3
  6.5 0.0 copy-start.1
  6.5 0.0 copy-start.4
  6.5 0.0 copy-start.5
  6.6 0.0 all-reduce.3.cloned.1.call-start
  6.6 4.6 %fusion.5 = f32[4,128,128]{1,2,0:T(8,128)} fusion(bf16[4,4096,128]{2,1,0:T(8,128)(2,1)} %param.9, s32[4,4096]{1,0:T(4,128)} %param.10), kind=kOutput, calls=%fused_computation.11 | convolution fusion | flops 538968064 | bytes 4521984 | tf_op jit(solution)/shard_map/scg,sck->sgk/dot_general | solution.py:22
  11.2 0.0 all-reduce.3.cloned.1.call-update
  11.2 0.0 all-gather.3.cloned.1.call-start
  11.3 0.0 copy-done.3
  11.3 0.2 fusion.18
  11.5 0.0 copy-done.2
  11.5 1.3 convert_reduce_fusion
  12.8 20.8 %all-reduce = (f32[4,128]{1,0:T(4,128)S(1)}, f32[32,32]{0,1:T(8,128)S(1)}) all-reduce(f32[4,128]{1,0:T(4,128)S(1)} %convert_reduce_fusion, f32[32,32]{0,1:T(8,128)S(1)} %fusion.18), channel_id=1, replica_groups=mesh['samp'=8,'pair'=16,'recv'=4] {'recv'}, use_global_device_ids=true, to_apply=%region_6.7 | all-reduce | flops 1536 | bytes 12288 | tf_op jit(solution)/shard_map/psum | solution.py:27
  33.6 38.7 %all-reduce.3.cloned.1.call-done = f32[4,128,128]{1,2,0:T(8,128)} async-done(((f32[4,128,128]{1,2,0:T(8,128)}), f32[4,128,128]{1,2,0:T(8,128)}) %all-reduce.3.cloned.1.call-update) | async-done | bytes 262160 | tf_op jit(solution)/shard_map/psum | solution.py:27
  72.3 1.7 divide_convert_fusion
  74.0 0.0 all-gather.3.cloned.1.call-update
  74.1 0.0 copy-done.1
  74.1 0.1 copy.24
  74.2 0.1 fusion.17
  74.3 34.7 %all-gather = f32[512,32]{1,0:T(8,128)S(1)} all-gather(f32[32,32]{1,0:T(8,128)S(1)} %fusion.17), channel_id=2, replica_groups=mesh['samp'=8,'pair'=16,'recv'=4] {'pair'}, dimensions={0}, use_global_device_ids=true | all-gather | bytes 69632 | tf_op jit(solution)/shard_map/all_gather | solution.py:56
  109.0 0.1 copy.16
  109.1 0.0 copy-done
  109.1 0.1 fusion.6
  109.2 0.1 copy.19
  109.3 2.9 cholesky.16
  112.3 0.6 compare_reduce_fusion
  112.9 0.7 fusion.8
  113.6 2.5 custom-call.10
  116.0 0.0 copy-done.4
  116.1 0.0 copy-done.5
  116.1 35.7 %all-gather.3.cloned.1.call-done = bf16[4,2048,128]{1,2,0:T(8,128)(2,1)} async-done(((bf16[4,128,128]{1,2,0:T(8,128)(2,1)}), bf16[4,2048,128]{1,2,0:T(8,128)(2,1)}) %all-gather.3.cloned.1.call-update) | async-done | bytes 2097168 | tf_op jit(solution)/shard_map/all_gather | solution.py:29
  151.8 2.0 fusion.3
  153.8 1.4 copy.21
  155.2 1.4 fusion.4
  156.6 2.5 copy.23
  159.1 0.7 gather_fusion
  159.8 2.3 gather_fusion.1
  162.2 0.3 multiply_reduce_fusion
  162.5 152.9 %psum.31 = f32[4,32]{1,0:T(4,128)S(1)} all-reduce(f32[4,32]{1,0:T(4,128)S(1)} %multiply_reduce_fusion), channel_id=1, replica_groups=mesh['samp'=8,'pair'=16,'recv'=4] {'pair','recv'}, use_global_device_ids=true, to_apply=%region_8.10 | all-reduce | flops 128 | bytes 1024 | tf_op jit(solution)/shard_map/psum | solution.py:55
  315.4 0.1 fusion.11
  315.5 0.7 fusion.9
  (10 shorter events, 0.1 us)
Async XLA Ops:
  6.5 102.6 %copy-start = (bf16[128,32]{0,1:T(8,128)(2,1)S(1)}, bf16[128,32]{0,1:T(8,128)(2,1)}, u32[]{:S(2)}) copy-start(bf16[128,32]{0,1:T(8,128)(2,1)} %param.14) | copy-start | bytes 24580
  6.5 4.9 %copy-start.2 = (s32[4,4096]{1,0:T(4,128)S(1)}, s32[4,4096]{1,0:T(4,128)}, u32[]{:S(2)}) copy-start(s32[4,4096]{1,0:T(4,128)} %param.10) | copy-start | bytes 196612
  6.5 4.7 %copy-start.3 = (bf16[32,32]{1,0:T(8,128)(2,1)S(1)}, bf16[32,32]{1,0:T(8,128)(2,1)}, u32[]{:S(2)}) copy-start(bf16[32,32]{1,0:T(8,128)(2,1)} %param.15) | copy-start | bytes 6148
  6.5 67.5 %copy-start.1 = (bf16[128,32]{0,1:T(8,128)(2,1)S(1)}, bf16[128,32]{0,1:T(8,128)(2,1)}, u32[]{:S(2)}) copy-start(bf16[128,32]{0,1:T(8,128)(2,1)} %param.13) | copy-start | bytes 24580
  6.5 109.5 %copy-start.4 = (s32[128]{0:T(128)S(1)}, s32[128]{0:T(128)}, u32[]{:S(2)}) copy-start(s32[128]{0:T(128)} %param.12) | copy-start | bytes 1540
  6.5 109.5 %copy-start.5 = (s32[128]{0:T(128)S(1)}, s32[128]{0:T(128)}, u32[]{:S(2)}) copy-start(s32[128]{0:T(128)} %param.11) | copy-start | bytes 1540
  6.6 65.7 %all-reduce.3.cloned.1.call-start = ((), (), s32[]{:S(2)}) async-start(), calls=%async_computation | async-start | bytes 524288 | tf_op jit(solution)/shard_map/psum | solution.py:27
  11.2 140.6 %all-gather.3.cloned.1.call-start = ((), (), s32[]{:S(2)}) async-start(), calls=%async_computation.1 | async-start | bytes 2228224 | tf_op jit(solution)/shard_map/all_gather | solution.py:29
Sparse Core Ops, SparseCore 0:
  11.4 60.8 all-reduce.2
  74.5 77.2 all-gather.2

commit v2 on v0

--- a/solution.py
+++ b/solution.py
@@ -52,7 +52,8 @@
     receiver_gram = jnp.einsum(
         "pr,pq->rq", receiver_factor, receiver_factor, preferred_element_type=jnp.float32
     )
-    product_total = lax.psum(partial_product, ("pair", "recv"))
+    inner = lax.psum(partial_product, "recv")
+    product_total = lax.psum(inner, "pair")
     pair_gram = lax.psum(pair_gram, "pair")
     receiver_gram = lax.psum(receiver_gram, "recv")
     hadamard = pair_gram * sender_gram * receiver_gram

time: 326 us -> 273 us (0.84)
  the two profiles are of different devices: /device:TPU:9 before, /device:TPU:64 now
where the time goes in v2:
time: 273 us
  waiting for transfers between devices  120 us (44%)
  blocking collectives  113 us (41%)
  between operations  13.6 us (5%)
  other arithmetic  10.1 us (4%)
  matrix products  9.45 us (3%)
  local copies, waits for them, and re-layouts  7.16 us (3%)
    psum x1, blocking collectives, body(): product_total = lax.psum(inner, 'pair')  79.5 us
    all_gather x1, waiting for transfers between devices, body(): segment = lax.all_gather(cluster_mean, 'pair', axis=1, tiled=True)  72.8 us
    psum x1, waiting for transfers between devices, body(): cluster_total, cell_count = lax.psum((part_sums, part_counts), 'recv')  47 us
    psum x1, blocking collectives, body(): inner = lax.psum(partial_product, 'recv')  18.1 us
    psum x1, blocking collectives, body(): cluster_total, cell_count = lax.psum((part_sums, part_counts), 'recv')  15.1 us
  transfers between devices with their start and end apart: 2, of which 2 were waited for; matrix products, arithmetic and copies ran while one was open for 1% of the time, Pallas kernels for 0%

profile of v2, /device:TPU:64, one launch (start us, length us, event | category | flops | bytes accessed | tf_op | source)
XLA Modules:
  0.0 272.8 jit_solution(14452679809832513594)
XLA Ops:
  6.5 0.0 copy-start
  6.5 0.0 copy-start.3
  6.5 0.0 copy-start.2
  6.5 0.0 copy-start.4
  6.5 0.0 copy-start.5
  6.5 0.0 copy-start.1
  6.6 0.0 all-reduce.4.cloned.1.call-start
  6.6 4.6 %fusion.3 = f32[4,128,128]{1,2,0:T(8,128)} fusion(bf16[4,4096,128]{2,1,0:T(8,128)(2,1)} %param.9, s32[4,4096]{1,0:T(4,128)} %param.10), kind=kOutput, calls=%fused_computation.9 | convolution fusion | flops 538968064 | bytes 4521984 | tf_op jit(solution)/shard_map/scg,sck->sgk/dot_general | solution.py:22
  11.2 0.0 all-reduce.4.cloned.1.call-update
  11.2 0.0 all-gather.2.cloned.1.call-start
  11.3 0.0 copy-done.3
  11.3 1.3 convert_reduce_fusion
  12.6 15.1 %psum.45 = f32[4,128]{1,0:T(4,128)S(1)} all-reduce(f32[4,128]{1,0:T(4,128)S(1)} %convert_reduce_fusion), channel_id=1, replica_groups=mesh['samp'=8,'pair'=16,'recv'=4] {'recv'}, use_global_device_ids=true, to_apply=%region_6.7 | all-reduce | flops 512 | bytes 4096 | tf_op jit(solution)/shard_map/psum | solution.py:27
  27.7 47.0 %all-reduce.4.cloned.1.call-done = f32[4,128,128]{1,2,0:T(8,128)} async-done(((f32[4,128,128]{1,2,0:T(8,128)}), f32[4,128,128]{1,2,0:T(8,128)}) %all-reduce.4.cloned.1.call-update) | async-done | bytes 262160 | tf_op jit(solution)/shard_map/psum | solution.py:27
  74.7 1.7 divide_convert_fusion
  76.4 0.0 all-gather.2.cloned.1.call-update
  76.5 0.0 copy-done.2
  76.5 0.1 copy.17
  76.6 0.0 copy-done.4
  76.6 0.0 copy-done.5
  76.7 0.1 fusion.15
  76.8 0.0 copy-done
  76.8 0.2 fusion.16
  77.0 72.8 %all-gather.2.cloned.1.call-done = bf16[4,2048,128]{1,2,0:T(8,128)(2,1)} async-done(((bf16[4,128,128]{1,2,0:T(8,128)(2,1)}), bf16[4,2048,128]{1,2,0:T(8,128)(2,1)}) %all-gather.2.cloned.1.call-update) | async-done | bytes 2097168 | tf_op jit(solution)/shard_map/all_gather | solution.py:29
  149.8 0.0 copy-done.1
  149.8 2.0 convolution_convert_fusion
  151.8 1.4 copy.23
  153.2 1.4 convolution_convert_fusion.1
  154.6 2.5 copy.24
  157.1 0.7 gather_fusion
  157.8 2.3 gather_fusion.1
  160.2 0.3 multiply_reduce_fusion
  160.5 18.1 %all-reduce.1 = (f32[4,32]{1,0:T(4,128)S(1)}, f32[32,32]{0,1:T(8,128)S(1)}) all-reduce(f32[4,32]{1,0:T(4,128)S(1)} %multiply_reduce_fusion, f32[32,32]{0,1:T(8,128)S(1)} %fusion.16), channel_id=1, replica_groups=mesh['samp'=8,'pair'=16,'recv'=4] {'recv'}, use_global_device_ids=true, to_apply=%region_8.10 | all-reduce | flops 1152 | bytes 9216 | tf_op jit(solution)/shard_map/psum | solution.py:55
  178.6 79.5 %all-reduce = (f32[4,32]{1,0:T(4,128)S(1)}, f32[32,32]{0,1:T(8,128)S(1)}) all-reduce(f32[4,32]{1,0:T(4,128)S(1)} %get-tuple-element.8, f32[32,32]{0,1:T(8,128)S(1)} %fusion.15), channel_id=1, replica_groups=mesh['samp'=8,'pair'=16,'recv'=4] {'pair'}, use_global_device_ids=true, to_apply=%region_9.11 | all-reduce | flops 1152 | bytes 9216 | tf_op jit(solution)/shard_map/psum | solution.py:56
  258.1 0.1 fusion.4
  258.2 0.1 copy.16
  258.3 2.9 %cholesky.16 = f32[32,32]{1,0:T(8,128)S(1)} custom-call(f32[32,32]{1,0:T(8,128)S(1)} %fusion.11), custom_call_target="Cholesky" | custom-call | tf_op jit(solution)/shard_map/jit(cholesky)/cholesky | solution.py:60
  261.2 0.6 compare_reduce_fusion
  261.9 0.7 fusion.6
  262.5 2.4 custom-call.10
  265.0 0.2 fusion.9
  265.2 0.8 fusion.7
  (9 shorter events, 0.1 us)
Async XLA Ops:
  6.5 70.3 %copy-start = (bf16[32,32]{1,0:T(8,128)(2,1)S(1)}, bf16[32,32]{1,0:T(8,128)(2,1)}, u32[]{:S(2)}) copy-start(bf16[32,32]{1,0:T(8,128)(2,1)} %param.15) | copy-start | bytes 6148
  6.5 4.8 %copy-start.3 = (s32[4,4096]{1,0:T(4,128)S(1)}, s32[4,4096]{1,0:T(4,128)}, u32[]{:S(2)}) copy-start(s32[4,4096]{1,0:T(4,128)} %param.10) | copy-start | bytes 196612
  6.5 69.9 %copy-start.2 = (bf16[128,32]{0,1:T(8,128)(2,1)S(1)}, bf16[128,32]{0,1:T(8,128)(2,1)}, u32[]{:S(2)}) copy-start(bf16[128,32]{0,1:T(8,128)(2,1)} %param.13) | copy-start | bytes 24580
  6.5 70.0 %copy-start.4 = (s32[128]{0:T(128)S(1)}, s32[128]{0:T(128)}, u32[]{:S(2)}) copy-start(s32[128]{0:T(128)} %param.12) | copy-start | bytes 1540
  6.5 70.1 %copy-start.5 = (s32[128]{0:T(128)S(1)}, s32[128]{0:T(128)}, u32[]{:S(2)}) copy-start(s32[128]{0:T(128)} %param.11) | copy-start | bytes 1540
  6.5 143.3 %copy-start.1 = (bf16[128,32]{0,1:T(8,128)(2,1)S(1)}, bf16[128,32]{0,1:T(8,128)(2,1)}, u32[]{:S(2)}) copy-start(bf16[128,32]{0,1:T(8,128)(2,1)} %param.14) | copy-start | bytes 24580
  6.6 68.1 %all-reduce.4.cloned.1.call-start = ((), (), s32[]{:S(2)}) async-start(), calls=%async_computation | async-start | bytes 524288 | tf_op jit(solution)/shard_map/psum | solution.py:27
  11.2 138.6 %all-gather.2.cloned.1.call-start = ((), (), s32[]{:S(2)}) async-start(), calls=%async_computation.1 | async-start | bytes 2228224 | tf_op jit(solution)/shard_map/all_gather | solution.py:29
Sparse Core Ops, SparseCore 0:
  11.4 63.2 all-reduce.3
  76.9 72.8 all-gather.1
